TPU v7x, 32 devices: a whole 2x2x4 slice. The times are simulated.
32 devices in a mesh: wa: 4 (over z), ha: 8 (over y, x, core).
Axes of the slice: x: 2, y: 2, z: 4, core: 2. Of those that a mesh axis runs over, the one named last changes fastest.
Arguments:
- tokens: bfloat16 [1024, 16384], P('ha', 'wa'), may hold values from -6 to 6
- gain_attn: bfloat16 [16384], P('wa'), may hold values from 0.25 to 1.75
- w_query: bfloat16 [16384, 16384], P('wa', 'ha'), may hold values from -0.046875 to 0.046875, as said below
- w_key: bfloat16 [16384, 1024], P('wa'), may hold values from -1.171875 to 1.171875, as said below
- w_value: bfloat16 [16384, 1024], P('wa'), may hold values from -0.046875 to 0.046875
- w_out: bfloat16 [16384, 16384], P('ha', 'wa'), may hold values from -0.1875 to 0.1875
- gain_ffn: bfloat16 [16384], P('wa'), may hold values from 0.25 to 1.75
- segment_ids: int32 [1024], replicated, may hold values from 0 to 31, never falling along the last dimension, each value on 1 to 256 neighbouring positions
Outputs:
- residual_out: bfloat16 [1024, 16384], P('ha', 'wa')
- ffn_input: bfloat16 [1024, 16384], P('ha', 'wa')
Inputs may be any that keep to these rules, and one draw needn't show every extreme that they name: `w_query`: entries scaled by 16384 ** -0.5. `w_key`: entries scaled by 16384 ** -0.5. `segment_ids`: segment ids never fall along the tokens; each prompt has 1 to 256 tokens and one has exactly 256.
All inputs are finite; a program needn't handle non-finite values.
Results may differ from a plain program's by a relative error of at most 0.00675.
The roundings to bfloat16 on the way count: a program that leaves them out, or rounds other values in their place, can miss the bound.
Values may be sent and summed in bfloat16 or wider, within the bound.
A program may use at most 192 MiB of HBM per device.

v0:
```python
import jax
import jax.numpy as jnp
from jax import lax
from jax.sharding import PartitionSpec as P

KVH = 8
HD = 128
WINDOW = 256
EPS = 1e-05


def rope_tables(position):
    half = HD // 2
    inverse = 500000.0 ** (-(jnp.arange(half, dtype=jnp.float32) * 2.0 / HD))
    angle = position[:, None] * inverse[None, :]
    return (jnp.cos(angle), jnp.sin(angle))


def rotate(values, cosine, sine):
    half = values.shape[-1] // 2
    first = values[..., :half]
    second = values[..., half:]
    cosine = cosine[:, None, :]
    sine = sine[:, None, :]
    return jnp.concatenate(
        [first * cosine - second * sine, second * cosine + first * sine], axis=-1
    )


def attend(queries, key_head, value_head, segment_ids, first):
    q_rows = queries.shape[0]
    size = min(WINDOW, q_rows)
    keys_pad = jnp.pad(key_head, ((WINDOW, 0), (0, 0)))
    values_pad = jnp.pad(value_head, ((WINDOW, 0), (0, 0)))
    segment_pad = jnp.pad(segment_ids, (WINDOW, 0), constant_values=-1)
    outs = []
    for at in range(0, q_rows, size):
        start = first + at
        query = queries[at : at + size]
        key = lax.dynamic_slice_in_dim(keys_pad, start, size + WINDOW, 0)
        value = lax.dynamic_slice_in_dim(values_pad, start, size + WINDOW, 0)
        k_segment = lax.dynamic_slice_in_dim(segment_pad, start, size + WINDOW, 0)
        q_segment = lax.dynamic_slice_in_dim(segment_ids, start, size, 0)
        k_at = jnp.arange(size + WINDOW, dtype=jnp.int32) - WINDOW
        q_at = jnp.arange(size, dtype=jnp.int32)
        allowed = (q_segment[:, None] == k_segment[None, :]) & (k_at[None, :] <= q_at[:, None])
        allowed = allowed & (k_at + start >= 0)[None, :]
        scores = jnp.einsum("thd,sd->hts", query, key, preferred_element_type=jnp.float32) * HD ** (
            -0.5
        )
        scores = jnp.where(allowed[None], scores, -1e30)
        peak = jnp.max(scores, axis=-1, keepdims=True)
        expo = jnp.where(allowed[None], jnp.exp(scores - peak), 0.0)
        weights = (expo / jnp.sum(expo, axis=-1, keepdims=True)).astype(jnp.bfloat16)
        out = jnp.einsum("hts,sd->thd", weights, value, preferred_element_type=jnp.float32)
        outs.append(out.astype(jnp.bfloat16))
    return jnp.concatenate(outs, axis=0)


def on_device(tokens, gain_attn, w_query, w_key, w_value, w_out, gain_ffn, segment_ids):
    rows_dev, width_dev = tokens.shape
    n_wa = lax.axis_size("wa")
    n_ha = lax.axis_size("ha")
    total = rows_dev * n_ha
    width = width_dev * n_wa
    head_cols = w_query.shape[1]
    heads_dev = head_cols // HD
    token_f = tokens.astype(jnp.float32)
    gain_one = gain_attn.astype(jnp.float32)
    kv_head = lax.axis_index("ha") // (n_ha // KVH)
    kv_weights = jnp.concatenate(
        [
            lax.dynamic_slice_in_dim(w_key, kv_head * HD, HD, 1),
            lax.dynamic_slice_in_dim(w_value, kv_head * HD, HD, 1),
        ],
        axis=1,
    )
    gathered = lax.all_gather(tokens, "ha", axis=0, tiled=True)
    gathered_f = gathered.astype(jnp.float32)
    row_sq = jnp.sum(gathered_f * gathered_f, axis=1)
    scaled = (gathered_f * gain_one).astype(jnp.bfloat16)
    kv_part = jnp.dot(scaled, kv_weights, preferred_element_type=jnp.float32)
    kv_sum = lax.psum(
        jnp.concatenate([kv_part, jnp.broadcast_to(row_sq[:, None], (total, HD))], axis=1), "wa"
    )
    row_scale = lax.rsqrt(kv_sum[:, 2 * HD] / width + EPS)
    index_all = jnp.arange(total, dtype=jnp.int32)
    fresh = jnp.concatenate([jnp.ones((1,), dtype=bool), segment_ids[1:] != segment_ids[:-1]])
    start_all = lax.cummax(jnp.where(fresh, index_all, jnp.zeros_like(index_all)), axis=0)
    cosine, sine = rope_tables((index_all - start_all).astype(jnp.float32))
    key_plain = (kv_sum[:, :HD] * row_scale[:, None]).astype(jnp.bfloat16)
    key_plain = lax.optimization_barrier(key_plain)
    value_head = (kv_sum[:, HD : 2 * HD] * row_scale[:, None]).astype(jnp.bfloat16)
    key_head = rotate(key_plain.astype(jnp.float32).reshape(total, 1, HD), cosine, sine)
    key_head = key_head.reshape(total, HD).astype(jnp.bfloat16)
    q_rows = total // n_wa
    first = lax.axis_index("wa") * q_rows
    block = scaled
    query_f = lax.psum_scatter(
        jnp.dot(block, w_query, preferred_element_type=jnp.float32),
        "wa",
        scatter_dimension=0,
        tiled=True,
    )
    q_scale = lax.dynamic_slice_in_dim(row_scale, first, q_rows, 0)
    q_cos = lax.dynamic_slice_in_dim(cosine, first, q_rows, 0)
    q_sin = lax.dynamic_slice_in_dim(sine, first, q_rows, 0)
    queries = rotate(
        (query_f * q_scale[:, None]).reshape(q_rows, heads_dev, HD), q_cos, q_sin
    ).astype(jnp.bfloat16)
    head_out = attend(queries, key_head, value_head, segment_ids, first)
    head_out = head_out.reshape(q_rows, head_cols)
    head_all = lax.all_gather(head_out, "wa", axis=0, tiled=True)
    block = head_all
    attended = lax.psum_scatter(
        jnp.dot(block, w_out, preferred_element_type=jnp.float32).astype(jnp.bfloat16),
        "ha",
        scatter_dimension=0,
        tiled=True,
    )
    residual_out = (token_f + attended.astype(jnp.float32)).astype(jnp.bfloat16)
    residual_f = residual_out.astype(jnp.float32)
    square_two = lax.psum(jnp.sum(residual_f * residual_f, axis=1), "wa")
    scale_two = lax.rsqrt(square_two / width + EPS)
    ffn_input = (residual_f * scale_two[:, None] * gain_ffn.astype(jnp.float32)).astype(
        jnp.bfloat16
    )
    return (residual_out, ffn_input)


def solution(mesh):
    in_specs = (
        P("ha", "wa"),
        P("wa"),
        P("wa", "ha"),
        P("wa", None),
        P("wa", None),
        P("ha", "wa"),
        P("wa"),
        P(),
    )
    out_specs = (P("ha", "wa"), P("ha", "wa"))
    return jax.shard_map(
        on_device, mesh=mesh, in_specs=in_specs, out_specs=out_specs, check_vma=False
    )
```

profile of v0, /device:TPU:0, one launch (start us, length us, event | category | flops | bytes accessed | tf_op | source)
XLA Modules:
  0.0 499.1 jit_solution(17607958058642940988)
XLA Ops:
  7.2 0.0 all-gather.3.cloned.1.call-start
  7.2 0.7 all-gather.3.cloned.1.call-update
  7.9 0.0 all-reduce.5.cloned.1.call-start
  7.9 0.7 convert_element_type.63
  8.7 1.7 constant_dynamic-slice_fusion.1
  10.3 56.5 %all-gather.3.cloned.1.call-done = bf16[1024,4096]{1,0:T(8,128)(2,1)} async-done(((bf16[128,4096]{1,0:T(8,128)(2,1)}), bf16[1024,4096]{1,0:T(8,128)(2,1)}) %all-gather.3.cloned.1.call-update) | async-done | bytes 8388624 | tf_op jit(solution)/shard_map/all_gather | solution.py:78
  66.9 5.2 %fusion.2 = f32[1024]{0:T(1024)S(1)} fusion(bf16[1024,4096]{1,0:T(8,128)(2,1)} %all-gather.3.cloned.1.call-done), kind=kLoop, calls=%fused_computation.4 | loop fusion | flops 12581888 | bytes 8392704 | tf_op jit(solution)/shard_map/reduce_sum | solution.py:80
  72.1 0.5 copy-done
  72.6 2.4 fusion.5
  75.1 1.3 pad_maximum_fusion
  76.4 0.0 all-reduce.5.cloned.1.call-update
  76.4 0.0 reduce-scatter.3.cloned.1.call-start
  76.5 24.1 %fusion.3 = f32[1024,2048]{1,0:T(8,128)} fusion(bf16[4096,2048]{1,0:T(8,128)(2,1)} %param.10, bf16[1024,4096]{1,0:T(8,128)(2,1)} %all-gather.3.cloned.1.call-done, f32[4096]{0:T(1024)S(1)} %convert_element_type.63), kind=kOutput, calls=%fused_computation.9 | convolution fusion | flops 17192452096 | bytes 33570816 | tf_op jit(solution)/shard_map/dot_general | solution.py:100
  100.6 0.0 reduce-scatter.3.cloned.1.call-update
  100.6 0.2 all-gather.5.cloned.1.call-start
  100.8 0.4 copy-done.3
  101.2 0.1 slice_compare_fusion
  101.3 0.1 add_select_fusion
  101.4 0.3 reduce-window.9
  101.7 0.1 slice.40
  101.8 0.1 dynamic_slice.32
  101.9 0.1 pad_dynamic-slice_fusion.2
  102.0 0.1 slice_reduce_fusion
  102.1 0.1 fusion.41
  102.2 0.2 broadcast_multiply_fusion
  102.4 0.5 dynamic-slice_cosine_fusion
  102.8 0.3 fusion.26
  103.1 42.5 %all-reduce.5.cloned.1.call-done = f32[1024,384]{0,1:T(8,128)} async-done(((f32[1024,384]{0,1:T(8,128)}), f32[1024,384]{0,1:T(8,128)}) %all-reduce.5.cloned.1.call-update) | async-done | bytes 1572880 | tf_op jit(solution)/shard_map/psum | solution.py:83
  145.6 0.8 fusion.40
  146.3 1.3 fusion.24
  147.7 1.2 fusion.32
  148.9 142.8 %reduce-scatter.3.cloned.1.call-done = f32[256,2048]{1,0:T(8,128)} async-done(((f32[1024,2048]{1,0:T(8,128)}), f32[256,2048]{1,0:T(8,128)}) %reduce-scatter.3.cloned.1.call-update) | async-done | bytes 2097168 | tf_op jit(solution)/shard_map/reduce_scatter | solution.py:99
  291.7 1.8 multiply_bitcast_fusion
  293.5 0.4 copy.23
  293.9 0.7 fusion.50
  294.6 1.4 subtract_convert_fusion
  296.0 1.3 fusion.19
  297.3 4.3 fusion.51
  301.6 1.7 fusion.18
  303.4 0.0 all-gather.5.cloned.1.call-update
  303.4 0.3 reduce-scatter.5.cloned.1.call-start
  303.7 81.0 %all-gather.5.cloned.1.call-done = bf16[1024,2048]{0,1:T(8,128)(2,1)} async-done(((bf16[256,2048]{0,1:T(8,128)(2,1)}), bf16[1024,2048]{0,1:T(8,128)(2,1)}) %all-gather.5.cloned.1.call-update) | async-done | bytes 4194320 | tf_op jit(solution)/shard_map/all_gather | solution.py:113
  384.7 23.2 %convolution_convert_fusion = bf16[1024,4096]{1,0:T(8,128)(2,1)} fusion(bf16[1024,2048]{0,1:T(8,128)(2,1)} %all-gather.5.cloned.1.call-done, bf16[2048,4096]{1,0:T(8,128)(2,1)} %param.13), kind=kOutput, calls=%fused_computation.8 | convolution fusion | flops 17184063488 | bytes 29360128 | tf_op jit(solution)/shard_map/dot_general | solution.py:116
  408.0 0.7 copy-done.4
  408.7 69.2 %reduce-scatter.5.cloned.1.call-done = bf16[128,4096]{1,0:T(8,128)(2,1)} async-done(((bf16[1024,4096]{1,0:T(8,128)(2,1)}), bf16[128,4096]{1,0:T(8,128)(2,1)}) %reduce-scatter.5.cloned.1.call-update) | async-done | bytes 1048592 | tf_op jit(solution)/shard_map/reduce_scatter | solution.py:115
  477.8 1.7 fusion.12
  479.5 11.7 %psum.15 = f32[128]{0:T(128)S(1)} all-reduce(f32[128]{0:T(128)S(1)} %get-tuple-element.2), channel_id=1, replica_groups=mesh['wa'=4,'ha'=8] {'wa'}, use_global_device_ids=true, to_apply=%region_9.10 | all-reduce | flops 128 | bytes 1024 | tf_op jit(solution)/shard_map/psum | solution.py:123
  491.2 1.3 fusion.14
  (17 shorter events, 0.2 us)
Async XLA Ops:
  7.2 59.7 %all-gather.3.cloned.1.call-start = ((), (), s32[]{:S(2)}) async-start(), calls=%async_computation.2 | async-start | bytes 9437184 | tf_op jit(solution)/shard_map/all_gather | solution.py:78
  7.9 137.7 %all-reduce.5.cloned.1.call-start = ((), (), s32[]{:S(2)}) async-start(), calls=%async_computation.3 | async-start | bytes 3145728 | tf_op jit(solution)/shard_map/psum | solution.py:83
  66.9 5.8 %copy-start = (bf16[1024,4096]{1,0:T(8,128)(2,1)S(1)}, bf16[1024,4096]{1,0:T(8,128)(2,1)}, u32[]{:S(2)}) copy-start(bf16[1024,4096]{1,0:T(8,128)(2,1)} %all-gather.3.cloned.1.call-done) | copy-start | bytes 25165828
  76.4 215.3 %reduce-scatter.3.cloned.1.call-start = ((), (), s32[]{:S(2)}) async-start(), calls=%async_computation.4 | async-start | bytes 10485760 | tf_op jit(solution)/shard_map/reduce_scatter | solution.py:99
  100.6 0.7 copy-start.3
  100.6 284.1 %all-gather.5.cloned.1.call-start = ((), (), s32[]{:S(2)}) async-start(), calls=%async_computation.5 | async-start | bytes 5242880 | tf_op jit(solution)/shard_map/all_gather | solution.py:113
  303.4 174.4 %reduce-scatter.5.cloned.1.call-start = ((), (), s32[]{:S(2)}) async-start(), calls=%async_computation.6 | async-start | bytes 9437184 | tf_op jit(solution)/shard_map/reduce_scatter | solution.py:115
  408.0 0.7 copy-start.4
  408.0 69.9 %copy-start.2 = (bf16[128,4096]{1,0:T(8,128)(2,1)S(1)}, bf16[128,4096]{1,0:T(8,128)(2,1)}, u32[]{:S(2)}) copy-start(bf16[128,4096]{1,0:T(8,128)(2,1)} %param.8) | copy-start | bytes 3145732
  479.5 13.0 %copy-start.1 = (bf16[128,4096]{1,0:T(8,128)(2,1)}, bf16[128,4096]{1,0:T(8,128)(2,1)S(1)}, u32[]{:S(2)}) copy-start(bf16[128,4096]{1,0:T(8,128)(2,1)S(1)} %get-tuple-element.3) | copy-start | bytes 3145732
Sparse Core Ops, SparseCore 0:
  9.9 56.9 all-gather.2
  76.6 68.9 all-reduce.4
  147.9 143.7 reduce-scatter.2
  303.5 81.1 all-gather.4
  408.1 69.6 reduce-scatter.4
where the time goes:
time: 499 us
  waiting for transfers between devices  393 us (79%)
  matrix products  52.8 us (11%)
  other arithmetic  22.1 us (4%)
  between operations  13.9 us (3%)
  blocking collectives  11.7 us (2%)
  local copies, waits for them, and re-layouts  5.19 us (1%)
    reduce_scatter x1, waiting for transfers between devices, on_device(): lax.psum_scatter(jnp.dot(block, w_query, preferred_element_type=jnp.float...  143 us
    all_gather x1, waiting for transfers between devices, on_device(): head_all = lax.all_gather(head_out, 'wa', axis=0, tiled=True)  81 us
    reduce_scatter x1, waiting for transfers between devices, on_device(): lax.psum_scatter(jnp.dot(block, w_out, preferred_element_type=jnp.float32...  69.2 us
    all_gather x1, waiting for transfers between devices, on_device(): gathered = lax.all_gather(tokens, 'ha', axis=0, tiled=True)  56.5 us
    psum x1, waiting for transfers between devices, on_device(): lax.psum(jnp.concatenate([kv_part, jnp.broadcast_to(row_sq[:, None], (tot...  42.5 us
    dot_general x1, matrix products, on_device(): jnp.dot(block, w_query, preferred_element_type=jnp.float32)  24.1 us
    dot_general x1, matrix products, on_device(): jnp.dot(block, w_out, preferred_element_type=jnp.float32)  23.2 us
    psum x1, blocking collectives, on_device(): square_two = lax.psum(jnp.sum(residual_f * residual_f, axis=1), 'wa')  11.7 us
  transfers between devices with their start and end apart: 5, of which 5 were waited for; matrix products, arithmetic and copies ran while one was open for 6% of the time, Pallas kernels for 0%

commit v1 on v0

--- a/solution.py
+++ b/solution.py
@@ -80,8 +80,11 @@
     row_sq = jnp.sum(gathered_f * gathered_f, axis=1)
     scaled = (gathered_f * gain_one).astype(jnp.bfloat16)
     kv_part = jnp.dot(scaled, kv_weights, preferred_element_type=jnp.float32)
-    kv_sum = lax.psum(
-        jnp.concatenate([kv_part, jnp.broadcast_to(row_sq[:, None], (total, HD))], axis=1), "wa"
+    kv_sum = jnp.sum(
+        lax.all_gather(
+            jnp.concatenate([kv_part, jnp.broadcast_to(row_sq[:, None], (total, HD))], axis=1), "wa"
+        ),
+        axis=0,
     )
     row_scale = lax.rsqrt(kv_sum[:, 2 * HD] / width + EPS)
     index_all = jnp.arange(total, dtype=jnp.int32)

time: 499 us -> 545 us (1.092)
  waiting for transfers between devices: 393 us -> 425 us
  local copies, waits for them, and re-layouts: 5.19 us -> 13.9 us
    all_gather x0 -> x1, waiting for transfers between devices: none -> 88.8 us  [on_device(): lax.all_gather(jnp.concatenate([kv_part, jnp.broadcast_to(row_sq[:, None]...]
    psum x1 -> x0, waiting for transfers between devices: 42.5 us -> none  [on_device(): lax.psum(jnp.concatenate([kv_part, jnp.broadcast_to(row_sq[:, None], (tot...]
    reduce_scatter x1, waiting for transfers between devices: 143 us -> 129 us  [on_device(): lax.psum_scatter(jnp.dot(block, w_query, preferred_element_type=jnp.float...]
    all_gather x0 -> x1, local copies, waits for them, and re-layouts: none -> 8.54 us  [on_device(): lax.all_gather(jnp.concatenate([kv_part, jnp.broadcast_to(row_sq[:, None]...]
    reduce_sum x0 -> x1, other arithmetic: none -> 6.61 us  [on_device(): jnp.sum(lax.all_gather(jnp.concatenate([kv_part, jnp.broadcast_to(row_sq[...]
  transfers between devices with their start and end apart: 5 -> 5, of which waited for: 5 -> 5; matrix products, arithmetic and copies ran while one was open for 6% -> 8% of each run, Pallas kernels for 0% -> 0%
where the time goes in v1:
time: 545 us
  waiting for transfers between devices  425 us (78%)
  matrix products  52.8 us (10%)
  other arithmetic  26.9 us (5%)
  local copies, waits for them, and re-layouts  13.9 us (3%)
  between operations  13.9 us (3%)
  blocking collectives  11.7 us (2%)
    reduce_scatter x1, waiting for transfers between devices, on_device(): lax.psum_scatter(jnp.dot(block, w_query, preferred_element_type=jnp.float...  129 us
    all_gather x1, waiting for transfers between devices, on_device(): lax.all_gather(jnp.concatenate([kv_part, jnp.broadcast_to(row_sq[:, None]...  88.8 us
    all_gather x1, waiting for transfers between devices, on_device(): head_all = lax.all_gather(head_out, 'wa', axis=0, tiled=True)  81.3 us
    reduce_scatter x1, waiting for transfers between devices, on_device(): lax.psum_scatter(jnp.dot(block, w_out, preferred_element_type=jnp.float32...  69.2 us
    all_gather x1, waiting for transfers between devices, on_device(): gathered = lax.all_gather(tokens, 'ha', axis=0, tiled=True)  56.5 us
    dot_general x1, matrix products, on_device(): jnp.dot(block, w_query, preferred_element_type=jnp.float32)  24.1 us
    dot_general x1, matrix products, on_device(): jnp.dot(block, w_out, preferred_element_type=jnp.float32)  23.2 us
    psum x1, blocking collectives, on_device(): square_two = lax.psum(jnp.sum(residual_f * residual_f, axis=1), 'wa')  11.7 us
  transfers between devices with their start and end apart: 5, of which 5 were waited for; matrix products, arithmetic and copies ran while one was open for 8% of the time, Pallas kernels for 0%

profile of v1, /device:TPU:0, one launch (start us, length us, event | category | flops | bytes accessed | tf_op | source)
XLA Modules:
  0.0 544.6 jit_solution(12266972876900854344)
XLA Ops:
  7.2 0.0 all-gather.5.cloned.1.call-start
  7.2 0.7 all-gather.5.cloned.1.call-update
  7.9 0.0 all-gather.9.cloned.1.call-start
  7.9 0.7 convert_element_type.63
  8.6 1.7 constant_dynamic-slice_fusion.1
  10.3 56.5 %all-gather.5.cloned.1.call-done = bf16[1024,4096]{1,0:T(8,128)(2,1)} async-done(((bf16[128,4096]{1,0:T(8,128)(2,1)}), bf16[1024,4096]{1,0:T(8,128)(2,1)}) %all-gather.5.cloned.1.call-update) | async-done | bytes 8388624 | tf_op jit(solution)/shard_map/all_gather | solution.py:78
  66.9 5.2 fusion.2
  72.1 0.5 copy-done
  72.6 2.4 fusion.5
  75.1 1.3 pad_maximum_fusion
  76.4 0.0 all-gather.9.cloned.1.call-update
  76.4 0.0 reduce-scatter.3.cloned.1.call-start
  76.5 24.1 %fusion.3 = f32[1024,2048]{1,0:T(8,128)} fusion(bf16[4096,2048]{1,0:T(8,128)(2,1)} %param.10, bf16[1024,4096]{1,0:T(8,128)(2,1)} %all-gather.5.cloned.1.call-done, f32[4096]{0:T(1024)S(1)} %convert_element_type.63), kind=kOutput, calls=%fused_computation.9 | convolution fusion | flops 17192452096 | bytes 33570816 | tf_op jit(solution)/shard_map/dot_general | solution.py:103
  100.6 0.0 reduce-scatter.3.cloned.1.call-update
  100.6 0.0 all-gather.7.cloned.1.call-start
  100.6 0.6 copy-done.3
  101.2 0.1 slice_compare_fusion
  101.3 0.1 add_select_fusion
  101.4 0.3 reduce-window.9
  101.7 0.1 slice.40
  101.8 0.1 dynamic_slice.32
  101.9 0.1 pad_dynamic-slice_fusion.2
  102.0 0.1 slice_reduce_fusion
  102.1 0.1 fusion.41
  102.2 0.2 broadcast_multiply_fusion
  102.4 0.5 dynamic-slice_cosine_fusion
  102.8 0.3 fusion.26
  103.1 88.8 %all-gather.9.cloned.1.call-done = f32[4096,384]{0,1:T(8,128)} async-done(((f32[1024,384]{0,1:T(8,128)}), f32[4096,384]{0,1:T(8,128)}) %all-gather.9.cloned.1.call-update) | async-done | bytes 6291472 | tf_op jit(solution)/shard_map/all_gather | solution.py:84
  191.9 8.5 %reshape.227 = f32[4,1024,384]{1,0,2:T(4,128)} reshape(f32[4096,384]{0,1:T(8,128)} %all-gather.9.cloned.1.call-done) | data formatting | bytes 12582912 | tf_op jit(solution)/shard_map/all_gather | solution.py:84
  200.5 6.6 %reduce_sum.37 = f32[1024,384]{0,1:T(8,128)S(1)} reduce(f32[4,1024,384]{1,0,2:T(4,128)} %reshape.227, f32[]{:T(128)} %constant.24.clone.1), dimensions={0}, to_apply=%region_1.2 | reduce | flops 1179648 | bytes 7864324 | tf_op jit(solution)/shard_map/reduce_sum | solution.py:83
  207.1 0.1 fusion.24
  207.3 1.2 fusion.32
  208.5 128.6 %reduce-scatter.3.cloned.1.call-done = f32[256,2048]{1,0:T(8,128)} async-done(((f32[1024,2048]{1,0:T(8,128)}), f32[256,2048]{1,0:T(8,128)}) %reduce-scatter.3.cloned.1.call-update) | async-done | bytes 2097168 | tf_op jit(solution)/shard_map/reduce_scatter | solution.py:102
  337.1 1.8 multiply_bitcast_fusion
  338.9 0.4 copy.33
  339.3 0.7 fusion.50
  340.0 1.4 subtract_convert_fusion
  341.3 1.3 fusion.19
  342.7 4.5 fusion.51
  347.2 1.7 fusion.18
  349.0 0.0 reduce-scatter.5.cloned.1.call-start
  349.0 81.3 %all-gather.7.cloned.1.call-done = bf16[1024,2048]{0,1:T(8,128)(2,1)} async-done(((bf16[256,2048]{0,1:T(8,128)(2,1)}), bf16[1024,2048]{0,1:T(8,128)(2,1)}) %all-gather.7.cloned.1.call-update) | async-done | bytes 4194320 | tf_op jit(solution)/shard_map/all_gather | solution.py:116
  430.3 23.2 %convolution_convert_fusion = bf16[1024,4096]{1,0:T(8,128)(2,1)} fusion(bf16[1024,2048]{0,1:T(8,128)(2,1)} %all-gather.7.cloned.1.call-done, bf16[2048,4096]{1,0:T(8,128)(2,1)} %param.13), kind=kOutput, calls=%fused_computation.8 | convolution fusion | flops 17184063488 | bytes 29360128 | tf_op jit(solution)/shard_map/dot_general | solution.py:119
  453.6 0.7 copy-done.4
  454.2 69.2 %reduce-scatter.5.cloned.1.call-done = bf16[128,4096]{1,0:T(8,128)(2,1)} async-done(((bf16[1024,4096]{1,0:T(8,128)(2,1)}), bf16[128,4096]{1,0:T(8,128)(2,1)}) %reduce-scatter.5.cloned.1.call-update) | async-done | bytes 1048592 | tf_op jit(solution)/shard_map/reduce_scatter | solution.py:118
  523.4 1.7 fusion.12
  525.1 11.7 %psum.7 = f32[128]{0:T(128)S(1)} all-reduce(f32[128]{0:T(128)S(1)} %get-tuple-element.2), channel_id=1, replica_groups=mesh['wa'=4,'ha'=8] {'wa'}, use_global_device_ids=true, to_apply=%region_9.10 | all-reduce | flops 128 | bytes 1024 | tf_op jit(solution)/shard_map/psum | solution.py:126
  536.8 1.3 fusion.14
  (19 shorter events, 0.2 us)
Async XLA Ops:
  7.2 59.7 %all-gather.5.cloned.1.call-start = ((), (), s32[]{:S(2)}) async-start(), calls=%async_computation.2 | async-start | bytes 9437184 | tf_op jit(solution)/shard_map/all_gather | solution.py:78
  7.9 184.0 %all-gather.9.cloned.1.call-start = ((), (), s32[]{:S(2)}) async-start(), calls=%async_computation.6 | async-start | bytes 7864320 | tf_op jit(solution)/shard_map/all_gather | solution.py:84
  66.9 5.8 %copy-start = (bf16[1024,4096]{1,0:T(8,128)(2,1)S(1)}, bf16[1024,4096]{1,0:T(8,128)(2,1)}, u32[]{:S(2)}) copy-start(bf16[1024,4096]{1,0:T(8,128)(2,1)} %all-gather.5.cloned.1.call-done) | copy-start | bytes 25165828
  76.4 260.7 %reduce-scatter.3.cloned.1.call-start = ((), (), s32[]{:S(2)}) async-start(), calls=%async_computation.3 | async-start | bytes 10485760 | tf_op jit(solution)/shard_map/reduce_scatter | solution.py:102
  100.6 0.7 copy-start.3
  100.6 329.7 %all-gather.7.cloned.1.call-start = ((), (), s32[]{:S(2)}) async-start(), calls=%async_computation.4 | async-start | bytes 5242880 | tf_op jit(solution)/shard_map/all_gather | solution.py:116
  349.0 174.4 %reduce-scatter.5.cloned.1.call-start = ((), (), s32[]{:S(2)}) async-start(), calls=%async_computation.5 | async-start | bytes 9437184 | tf_op jit(solution)/shard_map/reduce_scatter | solution.py:118
  453.5 0.7 copy-start.4
  453.5 69.9 %copy-start.2 = (bf16[128,4096]{1,0:T(8,128)(2,1)S(1)}, bf16[128,4096]{1,0:T(8,128)(2,1)}, u32[]{:S(2)}) copy-start(bf16[128,4096]{1,0:T(8,128)(2,1)} %param.8) | copy-start | bytes 3145732
  525.1 13.0 %copy-start.1 = (bf16[128,4096]{1,0:T(8,128)(2,1)}, bf16[128,4096]{1,0:T(8,128)(2,1)S(1)}, u32[]{:S(2)}) copy-start(bf16[128,4096]{1,0:T(8,128)(2,1)S(1)} %get-tuple-element.3) | copy-start | bytes 3145732
Sparse Core Ops, SparseCore 0:
  9.9 56.9 all-gather.4
  76.6 115.3 all-gather.8
  194.3 142.7 reduce-scatter.2
  349.1 81.1 all-gather.6
  453.7 69.6 reduce-scatter.4
